TPU v7x, 512 devices: a whole 4x4x16 slice. The times are simulated.
512 devices in a mesh: seq: 128 (over x, y, z_lo, core), head: 4 (over z_hi).
Axes of the slice: x: 4, y: 4, z: 16 (z_hi: 4, z_lo: 4; z = z_hi * 4 + z_lo), core: 2. Of those that a mesh axis runs over, the one named last changes fastest.
Arguments:
- queries: bfloat16 [16, 32768, 128], P('head', 'seq'), may hold values from -9 to 9
- key_vectors: bfloat16 [16, 32768, 128], P('head', 'seq'), may hold values from -9 to 9
- value_vectors: bfloat16 [16, 32768, 128], P('head', 'seq'), may hold values from -16 to 16
- block_perm: int32 [16, 64], P('head'), may hold values from 0 to 63, each once within a row
- out_weight: bfloat16 [16, 128, 2048], P('head'), may hold values from -0.125 to 0.125
- out_cotangent: bfloat16 [32768, 2048], P('seq', 'head'), may hold values from -6 to 6
Outputs:
- projected: bfloat16 [32768, 2048], P('seq', 'head')
- gradient_of_queries: bfloat16 [16, 32768, 128], P('head', 'seq')
- key_grad: bfloat16 [16, 32768, 128], P('head', 'seq')
- value_grad: bfloat16 [16, 32768, 128], P('head', 'seq')
Inputs may be any that keep to these rules, and one draw needn't show every extreme that they name: Each row of block_perm names every block of 0 to 63 once.
All inputs are finite; a program needn't handle non-finite values.
Results may differ from a plain program's by a relative error of at most 0.029.
Values may be sent and summed in bfloat16 or wider, within the bound.
A program may use at most 64 MiB of HBM per device.

v0:
```python
import math
import jax
import jax.numpy as jnp
from jax import lax
from jax.sharding import PartitionSpec as P


def partner(shard, axis, bit):
    return lax.ppermute(shard, axis, [(i, i ^ 1 << bit) for i in range(lax.axis_size(axis))])


def per_device(queries, key_vectors, value_vectors, block_perm, out_weight, out_cotangent):
    devices = lax.axis_size("seq")
    position = lax.axis_index("seq")
    parity = position % 2
    group_heads, tok_rows, head_width = queries.shape
    portion = tok_rows * head_width // devices
    score_scale = 1.0 / math.sqrt(head_width)
    owners = jnp.repeat(block_perm, 2, axis=1)
    indices = lax.iota(jnp.int32, devices)
    sources = [2 * owners, 2 * owners + 1]
    source_table = jnp.stack(sources, axis=1)
    slot_count = source_table.shape[1]
    select = (source_table[..., None] == indices).astype(jnp.bfloat16)
    stacked = jnp.stack([key_vectors, value_vectors])
    spread = lax.all_to_all(
        stacked.reshape(2, group_heads, devices, portion),
        "seq",
        split_axis=2,
        concat_axis=2,
        tiled=True,
    )
    picked = jnp.einsum(
        "hsij,chjl->chsil", select, spread, preferred_element_type=jnp.float32
    ).astype(jnp.bfloat16)
    routed = lax.all_to_all(picked, "seq", split_axis=3, concat_axis=3, tiled=True)
    routed = routed.reshape(2, group_heads, slot_count, tok_rows, head_width)
    partner_kv = routed.reshape(2, group_heads, 2 * tok_rows, head_width)
    pair_other = partner(stacked, "seq", 0)
    local_kv = jnp.where(
        parity == 0,
        jnp.concatenate([stacked, pair_other], 2),
        jnp.concatenate([pair_other, stacked], 2),
    )
    combined = jnp.concatenate([local_kv, partner_kv], 2)
    key_all = combined[0]
    value_all = combined[1]
    logit_scores = (
        jnp.einsum("htd,hkd->htk", queries, key_all, preferred_element_type=jnp.float32)
        * score_scale
    )
    row_max = jnp.max(logit_scores, axis=-1, keepdims=True)
    weights = jnp.exp(logit_scores - row_max)
    probabilities = weights / jnp.sum(weights, axis=-1, keepdims=True)
    reduced_probabilities = probabilities.astype(jnp.bfloat16)
    attention_result = jnp.einsum(
        "htk,hkd->htd", reduced_probabilities, value_all, preferred_element_type=jnp.float32
    ).astype(jnp.bfloat16)
    partial_out = jnp.einsum(
        "htd,hde->te", attention_result, out_weight, preferred_element_type=jnp.float32
    )
    summed = lax.psum(partial_out.astype(jnp.bfloat16), "head").astype(jnp.float32)
    columns = summed.shape[1] // lax.axis_size("head")
    result = lax.dynamic_slice_in_dim(summed, lax.axis_index("head") * columns, columns, 1)
    projected = result.astype(jnp.bfloat16)
    full_grad = lax.all_gather(out_cotangent, "head", axis=1, tiled=True)
    grad_att = jnp.einsum(
        "te,hde->htd", full_grad, out_weight, preferred_element_type=jnp.float32
    ).astype(jnp.bfloat16)
    row_delta = jnp.sum(
        grad_att.astype(jnp.float32) * attention_result.astype(jnp.float32), axis=-1, keepdims=True
    )
    probability_gradient = jnp.einsum(
        "htd,hkd->htk", grad_att, value_all, preferred_element_type=jnp.float32
    )
    score_gradient = (probabilities * (probability_gradient - row_delta) * score_scale).astype(
        jnp.bfloat16
    )
    gradient_of_queries = jnp.einsum(
        "htk,hkd->htd", score_gradient, key_all, preferred_element_type=jnp.float32
    ).astype(jnp.bfloat16)
    key_part = jnp.einsum(
        "htk,htd->hkd", score_gradient, queries, preferred_element_type=jnp.float32
    )
    value_part = jnp.einsum(
        "htk,htd->hkd", reduced_probabilities, grad_att, preferred_element_type=jnp.float32
    )
    gradients = jnp.stack([key_part, value_part])
    block_rows = 2 * tok_rows
    local_grad = gradients[:, :, :block_rows].reshape(2, group_heads, 2, tok_rows, head_width)
    own_grad = jnp.where(parity == 0, local_grad[:, :, 0], local_grad[:, :, 1])
    other_grad = jnp.where(parity == 0, local_grad[:, :, 1], local_grad[:, :, 0]).astype(
        jnp.bfloat16
    )
    partner_grad = gradients[:, :, block_rows:].reshape(2, group_heads, 2, tok_rows, head_width)
    partner_grad = partner_grad.astype(jnp.bfloat16)
    returned = lax.all_to_all(
        partner_grad.reshape(2, group_heads, slot_count, devices, portion),
        "seq",
        split_axis=3,
        concat_axis=3,
        tiled=True,
    )
    summed_back = jnp.einsum(
        "hsij,chsil->chjl", select, returned, preferred_element_type=jnp.float32
    ).astype(jnp.bfloat16)
    arrived = lax.all_to_all(summed_back, "seq", split_axis=2, concat_axis=2, tiled=True)
    arrived = arrived.reshape(2, group_heads, tok_rows, head_width).astype(jnp.float32)
    pair_back = partner(other_grad, "seq", 0).astype(jnp.float32)
    total_grad = own_grad + arrived + pair_back
    key_grad = total_grad[0].astype(jnp.bfloat16)
    value_grad = total_grad[1].astype(jnp.bfloat16)
    return (projected, gradient_of_queries, key_grad, value_grad)


def solution(mesh):
    return jax.shard_map(
        per_device,
        mesh=mesh,
        in_specs=(
            P("head", "seq", None),
            P("head", "seq", None),
            P("head", "seq", None),
            P("head", None),
            P("head", None, None),
            P("seq", "head"),
        ),
        out_specs=(
            P("seq", "head"),
            P("head", "seq", None),
            P("head", "seq", None),
            P("head", "seq", None),
        ),
        check_vma=False,
    )
```

profile of v0, /device:TPU:2, one launch (start us, length us, event | category | flops | bytes accessed | tf_op | source)
XLA Modules:
  0.0 314.9 jit_solution(3298835082028819904)
XLA Ops:
  7.2 1.2 stack.33
  8.4 1.0 stack.32
  9.5 1.3 copy.72
  10.8 13.0 %all-to-all-start = ((bf16[2,4,128,256]{3,0,1,2:T(2,128)(2,1)}), bf16[2,4,128,256]{3,0,1,2:T(2,128)(2,1)S(1)}, u32[]{:S(2)}, u32[]{:S(2)}) async-start(bf16[2,4,128,256]{3,0,1,2:T(2,128)(2,1)} %copy.72), calls=%async_computation | async-start | bytes 1048576 | tf_op jit(solution)/shard_map/all_to_all | solution.py:26
  24.1 16.4 %all-to-all-done = bf16[2,4,128,256]{3,0,1,2:T(2,128)(2,1)S(1)} async-done(((bf16[2,4,128,256]{3,0,1,2:T(2,128)(2,1)}), bf16[2,4,128,256]{3,0,1,2:T(2,128)(2,1)S(1)}, u32[]{:S(2)}, u32[]{:S(2)}) %all-to-all-start) | async-done | bytes 524320 | tf_op jit(solution)/shard_map/all_to_all | solution.py:26
  40.4 0.8 copy-done.14
  41.2 1.7 fusion.11
  42.9 2.1 copy.76
  45.0 9.3 %all-to-all-start.1 = ((bf16[2,4,2,128,256]{4,2,0,1,3:T(2,128)(2,1)}), bf16[2,4,2,128,256]{4,2,0,1,3:T(2,128)(2,1)}, u32[]{:S(2)}, u32[]{:S(2)}) async-start(bf16[2,4,2,128,256]{4,2,0,1,3:T(2,128)(2,1)} %copy.76), calls=%async_computation.1 | async-start | bytes 2097152 | tf_op jit(solution)/shard_map/all_to_all | solution.py:36
  54.5 2.2 collective-permute-start
  56.7 1.7 collective-permute-done
  58.4 1.6 maximum_select_fusion
  60.1 21.5 %all-to-all-done.1 = bf16[2,4,2,128,256]{4,2,0,1,3:T(2,128)(2,1)} async-done(((bf16[2,4,2,128,256]{4,2,0,1,3:T(2,128)(2,1)}), bf16[2,4,2,128,256]{4,2,0,1,3:T(2,128)(2,1)}, u32[]{:S(2)}, u32[]{:S(2)}) %all-to-all-start.1) | async-done | bytes 1048608 | tf_op jit(solution)/shard_map/all_to_all | solution.py:36
  81.6 2.5 copy.77
  84.1 2.3 reshape_reshape.3
  86.4 2.1 fusion.15
  88.5 4.6 %fusion.36 = (f32[4,256]{1,0:T(4,128)S(1)}, f32[4,256,1024]{1,2,0:T(8,128)}) fusion(bf16[4,1024,128]{2,1,0:T(8,128)(2,1)} %fusion.15, bf16[4,256,128]{2,1,0:T(8,128)(2,1)S(1)} %copy-done.15), kind=kOutput, calls=%fused_computation.63 | convolution fusion | flops 271582208 | bytes 5509120 | tf_op jit(solution)/shard_map/sub | solution.py:53
  93.1 2.6 fusion.10
  95.7 1.3 copy-done.3
  97.1 0.6 convolution_convert_fusion.3
  97.6 16.3 %all-gather.2.cloned.1.call-done = bf16[256,2048]{1,0:T(8,128)(2,1)} async-done(((bf16[256,512]{1,0:T(8,128)(2,1)}), bf16[256,2048]{1,0:T(8,128)(2,1)}) %all-gather.2.cloned.1.call-update) | async-done | bytes 1048592 | tf_op jit(solution)/shard_map/all_gather | solution.py:66
  113.9 2.1 fusion.22
  116.1 0.7 convolution_bitcast_fusion.1
  116.8 0.3 copy-done.11
  117.1 0.5 copy-done.7
  117.5 0.8 multiply_convert_fusion
  118.5 0.7 convolution_bitcast_fusion.2
  119.2 0.6 copy-done.8
  119.8 1.3 copy-done.2
  121.1 0.2 fusion.8
  121.3 1.3 convert_element_type.88
  122.5 2.3 copy.86
  124.8 45.1 %all_to_all.20 = bf16[2,4,2,128,256]{4,2,0,1,3:T(2,128)(2,1)S(1)} all-to-all(bf16[2,4,2,128,256]{4,2,0,1,3:T(2,128)(2,1)S(1)} %copy.86), channel_id=1, replica_groups=mesh['seq'=128,'head'=4] {'seq'}, dimensions={3} | all-to-all | bytes 2097152 | tf_op jit(solution)/shard_map/all_to_all | solution.py:97
  169.9 0.9 fusion.13
  170.8 1.1 copy.88
  171.9 8.6 %all-to-all-start.3 = ((bf16[2,4,128,256]{3,0,1,2:T(2,128)(2,1)}), bf16[2,4,128,256]{3,0,1,2:T(2,128)(2,1)S(1)}, u32[]{:S(2)}, u32[]{:S(2)}) async-start(bf16[2,4,128,256]{3,0,1,2:T(2,128)(2,1)} %copy.88), calls=%async_computation.3 | async-start | bytes 1048576 | tf_op jit(solution)/shard_map/all_to_all | solution.py:107
  180.6 1.8 fusion.6
  182.4 1.8 fusion.7
  184.3 1.3 copy-done.5
  185.5 0.9 fusion.21
  186.4 2.0 collective-permute-start.1
  188.5 1.6 convolution_convert_fusion.1
  190.1 111.2 %all-reduce.2.cloned.1.call-done = bf16[256,2048]{1,0:T(8,128)(2,1)} async-done(((bf16[256,2048]{1,0:T(8,128)(2,1)}), bf16[256,2048]{1,0:T(8,128)(2,1)}) %all-reduce.2.cloned.1.call-update) | async-done | bytes 1048592 | tf_op jit(solution)/shard_map/psum | solution.py:62
  301.3 1.7 convert_convert_fusion
  302.9 1.1 copy_convert_fusion
  304.0 1.3 reshape.55
  305.3 1.9 fusion.18
  307.3 0.8 slice_bitcast_fusion.2
  (43 shorter events, 0.6 us)
Async XLA Ops:
  7.2 106.8 %copy-start = (bf16[4,128,2048]{2,1,0:T(8,128)(2,1)S(1)}, bf16[4,128,2048]{2,1,0:T(8,128)(2,1)}, u32[]{:S(2)}) copy-start(bf16[4,128,2048]{2,1,0:T(8,128)(2,1)} %param.10) | copy-start | bytes 6291460
  7.2 16.6 %copy-start.17 = (s32[4,64]{1,0:T(4,128)S(1)}, s32[4,64]{1,0:T(4,128)}, u32[]{:S(2)}) copy-start(s32[4,64]{1,0:T(4,128)} %param.9) | copy-start | bytes 3076
  10.8 29.6 %all-to-all-start = ((bf16[2,4,128,256]{3,0,1,2:T(2,128)(2,1)}), bf16[2,4,128,256]{3,0,1,2:T(2,128)(2,1)S(1)}, u32[]{:S(2)}, u32[]{:S(2)}) async-start(bf16[2,4,128,256]{3,0,1,2:T(2,128)(2,1)} %copy.72), calls=%async_computation | async-start | bytes 1048576 | tf_op jit(solution)/shard_map/all_to_all | solution.py:26
  40.4 0.8 copy-start.14
  42.9 11.5 %copy-start.12 = (bf16[4,256,128]{2,1,0:T(8,128)(2,1)S(1)}, bf16[4,256,128]{2,1,0:T(8,128)(2,1)}, u32[]{:S(2)}) copy-start(bf16[4,256,128]{2,1,0:T(8,128)(2,1)} %param.8) | copy-start | bytes 786436
  45.0 9.4 %copy-start.13 = (bf16[4,256,128]{2,1,0:T(8,128)(2,1)S(1)}, bf16[4,256,128]{2,1,0:T(8,128)(2,1)}, u32[]{:S(2)}) copy-start(bf16[4,256,128]{2,1,0:T(8,128)(2,1)} %param.7) | copy-start | bytes 786436
  45.0 36.6 %all-to-all-start.1 = ((bf16[2,4,2,128,256]{4,2,0,1,3:T(2,128)(2,1)}), bf16[2,4,2,128,256]{4,2,0,1,3:T(2,128)(2,1)}, u32[]{:S(2)}, u32[]{:S(2)}) async-start(bf16[2,4,2,128,256]{4,2,0,1,3:T(2,128)(2,1)} %copy.76), calls=%async_computation.1 | async-start | bytes 2097152 | tf_op jit(solution)/shard_map/all_to_all | solution.py:36
  54.3 59.6 %all-gather.2.cloned.1.call-start = ((), (), s32[]{:S(2)}) async-start(), calls=%async_computation.5 | async-start | bytes 1310720 | tf_op jit(solution)/shard_map/all_gather | solution.py:66
  54.5 3.9 %collective-permute-start = (bf16[2,4,256,128]{3,2,1,0:T(8,128)(2,1)S(1)}, bf16[2,4,256,128]{3,2,1,0:T(8,128)(2,1)}, u32[]{:S(2)}, u32[]{:S(2)}) collective-permute-start(bf16[2,4,256,128]{3,2,1,0:T(8,128)(2,1)S(1)} %pad_maximum_fusion.2), channel_id=1, source_target_pairs={{0,4},{4,0},{8,12},{12,8},{16,20},{20,16},{24,28},{28,24},{32,36},... | collective-permute-start | bytes 1572872 | tf_op jit(solution)/shard_map/ppermute | solution.py:9
  86.4 2.1 copy-start.15
  93.1 4.0 %copy-start.6 = (bf16[2,4,512,128]{3,2,1,0:T(8,128)(2,1)S(1)}, bf16[2,4,512,128]{3,2,1,0:T(8,128)(2,1)}, u32[]{:S(2)}) copy-start(bf16[2,4,512,128]{3,2,1,0:T(8,128)(2,1)} %reshape_reshape.3) | copy-start | bytes 3145732
  95.7 1.3 copy-start.3
  113.9 2.1 copy-start.4
  113.9 3.1 copy-start.11
  116.1 1.5 copy-start.7
  116.8 2.4 copy-start.1
  117.5 0.9 copy-start.16
  118.5 1.3 copy-start.8
  119.8 1.3 copy-start.2
  171.9 131.0 %all-to-all-start.3 = ((bf16[2,4,128,256]{3,0,1,2:T(2,128)(2,1)}), bf16[2,4,128,256]{3,0,1,2:T(2,128)(2,1)S(1)}, u32[]{:S(2)}, u32[]{:S(2)}) async-start(bf16[2,4,128,256]{3,0,1,2:T(2,128)(2,1)} %copy.88), calls=%async_computation.3 | async-start | bytes 1048576 | tf_op jit(solution)/shard_map/all_to_all | solution.py:107
  180.5 120.8 %all-reduce.2.cloned.1.call-start = ((), (), s32[]{:S(2)}) async-start(), calls=%async_computation.4 | async-start | bytes 2097152 | tf_op jit(solution)/shard_map/psum | solution.py:62
  182.4 6.1 %copy-start.9 = (bf16[4,256,1024]{1,2,0:T(8,128)(2,1)S(1)}, bf16[4,256,1024]{1,2,0:T(8,128)(2,1)}, u32[]{:S(2)}) copy-start(bf16[4,256,1024]{1,2,0:T(8,128)(2,1)} %copy-done.8) | copy-start | bytes 6291460
  182.4 6.1 %copy-start.10 = (bf16[4,1024,128]{2,1,0:T(8,128)(2,1)S(1)}, bf16[4,1024,128]{2,1,0:T(8,128)(2,1)}, u32[]{:S(2)}) copy-start(bf16[4,1024,128]{2,1,0:T(8,128)(2,1)} %fusion.15) | copy-start | bytes 3145732
  184.2 1.3 copy-start.5
  186.4 118.9 %collective-permute-start.1 = (bf16[2,4,256,128]{3,2,1,0:T(8,128)(2,1)}, bf16[2,4,256,128]{3,2,1,0:T(8,128)(2,1)}, u32[]{:S(2)}, u32[]{:S(2)}) collective-permute-start(bf16[2,4,256,128]{3,2,1,0:T(8,128)(2,1)} %fusion.21), channel_id=1, source_target_pairs={{0,4},{4,0},{8,12},{12,8},{16,20},{20,16},{24,28},{28,24},{32,36},... | collective-permute-start | bytes 1572872 | tf_op jit(solution)/shard_map/ppermute | solution.py:9
Sparse Core Ops, SparseCore 0:
  57.3 56.6 all-gather.1
  184.3 116.9 all-reduce.1
where the time goes:
time: 316 us; the launch traced here: 315 us
  waiting for transfers between devices  167 us (53%)
  blocking collectives  45.1 us (14%)
  starting transfers between devices  35.3 us (11%)
  local copies, waits for them, and re-layouts  23.7 us (8%)
  matrix products  15.4 us (5%)
  between operations  14.4 us (5%)
  other arithmetic  14.1 us (4%)
    psum x1, waiting for transfers between devices, per_device(): lax.psum(partial_out.astype(jnp.bfloat16), 'head').astype(jnp.float32)  111 us
    all_to_all x1, blocking collectives, per_device(): lax.all_to_all(partner_grad.reshape(2, group_heads, slot_count, devices,...  45.1 us
    all_to_all x1, waiting for transfers between devices, per_device(): lax.all_to_all(picked, 'seq', split_axis=3, concat_axis=3, tiled=True)  21.5 us
    all_to_all x1, waiting for transfers between devices, per_device(): lax.all_to_all(stacked.reshape(2, group_heads, devices, portion), 'seq',...  16.4 us
    all_gather x1, waiting for transfers between devices, per_device(): full_grad = lax.all_gather(out_cotangent, 'head', axis=1, tiled=True)  16.3 us
    all_to_all x1, starting transfers between devices, per_device(): lax.all_to_all(stacked.reshape(2, group_heads, devices, portion), 'seq',...  13 us
    all_to_all x1, starting transfers between devices, per_device(): lax.all_to_all(picked, 'seq', split_axis=3, concat_axis=3, tiled=True)  9.32 us
    all_to_all x1, starting transfers between devices, per_device(): lax.all_to_all(summed_back, 'seq', split_axis=2, concat_axis=2, tiled=True)  8.6 us
  transfers between devices with their start and end apart: 7, of which 5 were waited for; matrix products, arithmetic and copies ran while one was open for 8% of the time, Pallas kernels for 0%

commit v1 on v0

--- a/solution.py
+++ b/solution.py
@@ -59,7 +59,9 @@
     partial_out = jnp.einsum(
         "htd,hde->te", attention_result, out_weight, preferred_element_type=jnp.float32
     )
-    summed = lax.psum(partial_out.astype(jnp.bfloat16), "head").astype(jnp.float32)
+    summed = jnp.sum(lax.all_gather(partial_out.astype(jnp.bfloat16), "head"), axis=0).astype(
+        jnp.float32
+    )
     columns = summed.shape[1] // lax.axis_size("head")
     result = lax.dynamic_slice_in_dim(summed, lax.axis_index("head") * columns, columns, 1)
     projected = result.astype(jnp.bfloat16)

time: 316 us -> 341 us (1.079)
  the two profiles are of different devices: /device:TPU:2 before, /device:TPU:1 now
where the time goes in v1:
time: 341 us; the launch traced here: 340 us
  waiting for transfers between devices  142 us (42%)
  starting transfers between devices  125 us (37%)
  local copies, waits for them, and re-layouts  25.9 us (8%)
  other arithmetic  16.3 us (5%)
  matrix products  16.1 us (5%)
  between operations  14.4 us (4%)
    all_to_all x1, starting transfers between devices, per_device(): lax.all_to_all(summed_back, 'seq', split_axis=2, concat_axis=2, tiled=True)  82 us
    all_to_all x1, waiting for transfers between devices, per_device(): lax.all_to_all(summed_back, 'seq', split_axis=2, concat_axis=2, tiled=True)  51.2 us
    all_to_all x1, waiting for transfers between devices, per_device(): lax.all_to_all(partner_grad.reshape(2, group_heads, slot_count, devices,...  32.5 us
    all_to_all x1, waiting for transfers between devices, per_device(): lax.all_to_all(picked, 'seq', split_axis=3, concat_axis=3, tiled=True)  22.8 us
    all_to_all x1, waiting for transfers between devices, per_device(): lax.all_to_all(stacked.reshape(2, group_heads, devices, portion), 'seq',...  18 us
    all_gather x1, waiting for transfers between devices, per_device(): full_grad = lax.all_gather(out_cotangent, 'head', axis=1, tiled=True)  16.3 us
    all_to_all x1, starting transfers between devices, per_device(): lax.all_to_all(partner_grad.reshape(2, group_heads, slot_count, devices,...  15.9 us
    all_to_all x1, starting transfers between devices, per_device(): lax.all_to_all(stacked.reshape(2, group_heads, devices, portion), 'seq',...  13.8 us
  transfers between devices with their start and end apart: 8, of which 6 were waited for; matrix products, arithmetic and copies ran while one was open for 9% of the time, Pallas kernels for 0%

profile of v1, /device:TPU:1, one launch (start us, length us, event | category | flops | bytes accessed | tf_op | source)
XLA Modules:
  0.0 340.4 jit_solution(4021444114260147889)
XLA Ops:
  7.2 1.2 stack.32
  8.4 1.0 stack.33
  9.5 1.3 copy.72
  10.8 13.8 %all-to-all-start = ((bf16[2,4,128,256]{3,0,1,2:T(2,128)(2,1)}), bf16[2,4,128,256]{3,0,1,2:T(2,128)(2,1)S(1)}, u32[]{:S(2)}, u32[]{:S(2)}) async-start(bf16[2,4,128,256]{3,0,1,2:T(2,128)(2,1)} %copy.72), calls=%async_computation | async-start | bytes 1048576 | tf_op jit(solution)/shard_map/all_to_all | solution.py:26
  24.9 18.0 %all-to-all-done = bf16[2,4,128,256]{3,0,1,2:T(2,128)(2,1)S(1)} async-done(((bf16[2,4,128,256]{3,0,1,2:T(2,128)(2,1)}), bf16[2,4,128,256]{3,0,1,2:T(2,128)(2,1)S(1)}, u32[]{:S(2)}, u32[]{:S(2)}) %all-to-all-start) | async-done | bytes 524320 | tf_op jit(solution)/shard_map/all_to_all | solution.py:26
  43.0 0.8 copy-done.14
  43.8 1.7 fusion.11
  45.5 2.1 copy.76
  47.5 7.5 %all-to-all-start.1 = ((bf16[2,4,2,128,256]{4,2,0,1,3:T(2,128)(2,1)}), bf16[2,4,2,128,256]{4,2,0,1,3:T(2,128)(2,1)}, u32[]{:S(2)}, u32[]{:S(2)}) async-start(bf16[2,4,2,128,256]{4,2,0,1,3:T(2,128)(2,1)} %copy.76), calls=%async_computation.1 | async-start | bytes 2097152 | tf_op jit(solution)/shard_map/all_to_all | solution.py:36
  55.2 3.2 collective-permute-start
  58.4 1.4 collective-permute-done
  59.9 1.7 maximum_select_fusion
  61.6 22.8 %all-to-all-done.1 = bf16[2,4,2,128,256]{4,2,0,1,3:T(2,128)(2,1)} async-done(((bf16[2,4,2,128,256]{4,2,0,1,3:T(2,128)(2,1)}), bf16[2,4,2,128,256]{4,2,0,1,3:T(2,128)(2,1)}, u32[]{:S(2)}, u32[]{:S(2)}) %all-to-all-start.1) | async-done | bytes 1048608 | tf_op jit(solution)/shard_map/all_to_all | solution.py:36
  84.4 2.6 copy.77
  87.0 2.3 reshape_reshape.3
  89.3 2.1 fusion.15
  91.4 4.6 %fusion.36 = (f32[4,256]{1,0:T(4,128)S(1)}, f32[4,256,1024]{1,2,0:T(8,128)}) fusion(bf16[4,1024,128]{2,1,0:T(8,128)(2,1)} %fusion.15, bf16[4,256,128]{2,1,0:T(8,128)(2,1)S(1)} %copy-done.15), kind=kOutput, calls=%fused_computation.63 | convolution fusion | flops 271582208 | bytes 5509120 | tf_op jit(solution)/shard_map/sub | solution.py:53
  96.0 2.6 fusion.10
  98.7 1.3 copy-done.3
  100.0 0.6 convolution_convert_fusion.3
  100.6 16.3 %all-gather.4.cloned.1.call-done = bf16[256,2048]{1,0:T(8,128)(2,1)} async-done(((bf16[256,512]{1,0:T(8,128)(2,1)}), bf16[256,2048]{1,0:T(8,128)(2,1)}) %all-gather.4.cloned.1.call-update) | async-done | bytes 1048592 | tf_op jit(solution)/shard_map/all_gather | solution.py:68
  116.9 2.1 fusion.22
  119.1 0.7 convolution_bitcast_fusion.1
  120.1 0.5 copy-done.7
  120.5 0.8 multiply_convert_fusion
  121.5 0.7 convolution_bitcast_fusion.2
  122.2 0.6 copy-done.8
  122.8 1.4 copy-done.2
  124.4 1.2 convert_element_type.90
  125.6 3.3 copy.86
  128.9 15.9 %all-to-all-start.2 = ((bf16[2,4,2,128,256]{4,2,0,1,3:T(2,128)(2,1)}), bf16[2,4,2,128,256]{4,2,0,1,3:T(2,128)(2,1)S(1)}, u32[]{:S(2)}, u32[]{:S(2)}) async-start(bf16[2,4,2,128,256]{4,2,0,1,3:T(2,128)(2,1)} %copy.86), calls=%async_computation.2 | async-start | bytes 2097152 | tf_op jit(solution)/shard_map/all_to_all | solution.py:99
  144.9 1.7 fusion.6
  146.7 32.5 %all-to-all-done.2 = bf16[2,4,2,128,256]{4,2,0,1,3:T(2,128)(2,1)S(1)} async-done(((bf16[2,4,2,128,256]{4,2,0,1,3:T(2,128)(2,1)}), bf16[2,4,2,128,256]{4,2,0,1,3:T(2,128)(2,1)S(1)}, u32[]{:S(2)}, u32[]{:S(2)}) %all-to-all-start.2) | async-done | bytes 1048608 | tf_op jit(solution)/shard_map/all_to_all | solution.py:99
  179.2 1.6 fusion.13
  180.9 2.0 copy.88
  182.9 82.0 %all-to-all-start.3 = ((bf16[2,4,128,256]{3,0,1,2:T(2,128)(2,1)}), bf16[2,4,128,256]{3,0,1,2:T(2,128)(2,1)S(1)}, u32[]{:S(2)}, u32[]{:S(2)}) async-start(bf16[2,4,128,256]{3,0,1,2:T(2,128)(2,1)} %copy.88), calls=%async_computation.3 | async-start | bytes 1048576 | tf_op jit(solution)/shard_map/all_to_all | solution.py:109
  265.0 1.8 fusion.7
  266.8 1.4 copy-done.5
  268.2 0.9 fusion.21
  269.1 2.8 collective-permute-start.1
  271.9 1.6 convolution_convert_fusion.1
  273.5 51.2 %all-to-all-done.3 = bf16[2,4,128,256]{3,0,1,2:T(2,128)(2,1)S(1)} async-done(((bf16[2,4,128,256]{3,0,1,2:T(2,128)(2,1)}), bf16[2,4,128,256]{3,0,1,2:T(2,128)(2,1)S(1)}, u32[]{:S(2)}, u32[]{:S(2)}) %all-to-all-start.3) | async-done | bytes 524320 | tf_op jit(solution)/shard_map/all_to_all | solution.py:109
  324.6 1.1 copy_convert_fusion
  325.8 1.3 reshape.55
  327.1 1.9 fusion.18
  329.0 0.8 slice_bitcast_fusion.2
  329.8 3.1 reduce_sum.31
  332.9 0.7 convert_convert_fusion
  (45 shorter events, 1.1 us)
Async XLA Ops:
  7.2 109.8 %copy-start = (bf16[4,128,2048]{2,1,0:T(8,128)(2,1)S(1)}, bf16[4,128,2048]{2,1,0:T(8,128)(2,1)}, u32[]{:S(2)}) copy-start(bf16[4,128,2048]{2,1,0:T(8,128)(2,1)} %param.10) | copy-start | bytes 6291460
  7.2 17.5 %copy-start.17 = (s32[4,64]{1,0:T(4,128)S(1)}, s32[4,64]{1,0:T(4,128)}, u32[]{:S(2)}) copy-start(s32[4,64]{1,0:T(4,128)} %param.9) | copy-start | bytes 3076
  10.8 32.1 %all-to-all-start = ((bf16[2,4,128,256]{3,0,1,2:T(2,128)(2,1)}), bf16[2,4,128,256]{3,0,1,2:T(2,128)(2,1)S(1)}, u32[]{:S(2)}, u32[]{:S(2)}) async-start(bf16[2,4,128,256]{3,0,1,2:T(2,128)(2,1)} %copy.72), calls=%async_computation | async-start | bytes 1048576 | tf_op jit(solution)/shard_map/all_to_all | solution.py:26
  43.0 0.8 copy-start.14
  45.4 9.7 %copy-start.12 = (bf16[4,256,128]{2,1,0:T(8,128)(2,1)S(1)}, bf16[4,256,128]{2,1,0:T(8,128)(2,1)}, u32[]{:S(2)}) copy-start(bf16[4,256,128]{2,1,0:T(8,128)(2,1)} %param.8) | copy-start | bytes 786436
  47.5 7.6 %copy-start.13 = (bf16[4,256,128]{2,1,0:T(8,128)(2,1)S(1)}, bf16[4,256,128]{2,1,0:T(8,128)(2,1)}, u32[]{:S(2)}) copy-start(bf16[4,256,128]{2,1,0:T(8,128)(2,1)} %param.7) | copy-start | bytes 786436
  47.5 36.8 %all-to-all-start.1 = ((bf16[2,4,2,128,256]{4,2,0,1,3:T(2,128)(2,1)}), bf16[2,4,2,128,256]{4,2,0,1,3:T(2,128)(2,1)}, u32[]{:S(2)}, u32[]{:S(2)}) async-start(bf16[2,4,2,128,256]{4,2,0,1,3:T(2,128)(2,1)} %copy.76), calls=%async_computation.1 | async-start | bytes 2097152 | tf_op jit(solution)/shard_map/all_to_all | solution.py:36
  55.1 61.8 %all-gather.4.cloned.1.call-start = ((), (), s32[]{:S(2)}) async-start(), calls=%async_computation.4 | async-start | bytes 1310720 | tf_op jit(solution)/shard_map/all_gather | solution.py:68
  55.2 4.6 %collective-permute-start = (bf16[2,4,256,128]{3,2,1,0:T(8,128)(2,1)S(1)}, bf16[2,4,256,128]{3,2,1,0:T(8,128)(2,1)}, u32[]{:S(2)}, u32[]{:S(2)}) collective-permute-start(bf16[2,4,256,128]{3,2,1,0:T(8,128)(2,1)S(1)} %pad_maximum_fusion.2), channel_id=1, source_target_pairs={{0,4},{4,0},{8,12},{12,8},{16,20},{20,16},{24,28},{28,24},{32,36},... | collective-permute-start | bytes 1572872 | tf_op jit(solution)/shard_map/ppermute | solution.py:9
  89.3 2.2 copy-start.15
  96.0 4.0 %copy-start.6 = (bf16[2,4,512,128]{3,2,1,0:T(8,128)(2,1)S(1)}, bf16[2,4,512,128]{3,2,1,0:T(8,128)(2,1)}, u32[]{:S(2)}) copy-start(bf16[2,4,512,128]{3,2,1,0:T(8,128)(2,1)} %reshape_reshape.3) | copy-start | bytes 3145732
  98.7 1.3 copy-start.3
  116.9 2.1 copy-start.4
  116.9 3.1 copy-start.11
  119.1 1.5 copy-start.7
  119.8 2.4 copy-start.1
  120.5 0.9 copy-start.16
  121.5 1.3 copy-start.8
  122.8 1.4 copy-start.2
  128.9 50.3 %all-to-all-start.2 = ((bf16[2,4,2,128,256]{4,2,0,1,3:T(2,128)(2,1)}), bf16[2,4,2,128,256]{4,2,0,1,3:T(2,128)(2,1)S(1)}, u32[]{:S(2)}, u32[]{:S(2)}) async-start(bf16[2,4,2,128,256]{4,2,0,1,3:T(2,128)(2,1)} %copy.86), calls=%async_computation.2 | async-start | bytes 2097152 | tf_op jit(solution)/shard_map/all_to_all | solution.py:99
  144.9 184.9 %all-gather.6.cloned.1.call-start = ((), (), s32[]{:S(2)}) async-start(), calls=%async_computation.5 | async-start | bytes 5242880 | tf_op jit(solution)/shard_map/all_gather | solution.py:62
  182.9 141.8 %all-to-all-start.3 = ((bf16[2,4,128,256]{3,0,1,2:T(2,128)(2,1)}), bf16[2,4,128,256]{3,0,1,2:T(2,128)(2,1)S(1)}, u32[]{:S(2)}, u32[]{:S(2)}) async-start(bf16[2,4,128,256]{3,0,1,2:T(2,128)(2,1)} %copy.88), calls=%async_computation.3 | async-start | bytes 1048576 | tf_op jit(solution)/shard_map/all_to_all | solution.py:109
  264.9 7.0 %copy-start.9 = (bf16[4,256,1024]{1,2,0:T(8,128)(2,1)S(1)}, bf16[4,256,1024]{1,2,0:T(8,128)(2,1)}, u32[]{:S(2)}) copy-start(bf16[4,256,1024]{1,2,0:T(8,128)(2,1)} %copy-done.8) | copy-start | bytes 6291460
  264.9 7.0 %copy-start.10 = (bf16[4,1024,128]{2,1,0:T(8,128)(2,1)S(1)}, bf16[4,1024,128]{2,1,0:T(8,128)(2,1)}, u32[]{:S(2)}) copy-start(bf16[4,1024,128]{2,1,0:T(8,128)(2,1)} %fusion.15) | copy-start | bytes 3145732
  266.8 1.4 copy-start.5
  269.1 58.0 %collective-permute-start.1 = (bf16[2,4,256,128]{3,2,1,0:T(8,128)(2,1)}, bf16[2,4,256,128]{3,2,1,0:T(8,128)(2,1)}, u32[]{:S(2)}, u32[]{:S(2)}) collective-permute-start(bf16[2,4,256,128]{3,2,1,0:T(8,128)(2,1)} %fusion.21), channel_id=1, source_target_pairs={{0,4},{4,0},{8,12},{12,8},{16,20},{20,16},{24,28},{28,24},{32,36},... | collective-permute-start | bytes 1572872 | tf_op jit(solution)/shard_map/ppermute | solution.py:9
Sparse Core Ops, SparseCore 0:
  58.5 58.3 all-gather.3
  147.8 112.8 all-gather.5
